TPU v7x, 512 devices: a whole 4x8x8 slice. The times are simulated.
512 devices in a mesh: dp: 16 (over z, core), cls: 32 (over x, y).
Axes of the slice: x: 4, y: 8, z: 8, core: 2. Of those that a mesh axis runs over, the one named last changes fastest.
Arguments:
- embeddings: bfloat16 [131072, 768], P(('dp', 'cls'))
- class_rows: bfloat16 [128, 256, 768], P('cls')
- cand_blocks: int32 [1024, 8], P(('dp', 'cls')), may hold values from 0 to 127, all different within a row; in each aligned block of 64 rows (0 to 63, 64 to 127, ...) at most 8 rows name the same one
- label_pos: int32 [131072], P(('dp', 'cls')), may hold values from 0 to 2047
Outputs:
- image_loss: float32 [131072], P('dp')
- class_grad: float32 [256, 128, 768], P('dp', 'cls')
Inputs may be any that keep to these rules, and one draw needn't show every extreme that they name: `cand_blocks`: the 8 blocks of one list differ; block n lives on index n // 4 of cls. Among the 64 lists of one index of dp no block is named by more than 8 lists, and in some index of dp one block is named by exactly 8.
All inputs are finite; a program needn't handle non-finite values.
Results may differ from a plain program's by a relative error of at most 0.00099.
Values may be sent and summed in bfloat16 or wider, within the bound.
A program may use at most 64 MiB of HBM per device.

v0:
```python
import jax
import jax.numpy as jnp
from jax import lax
from jax.sharding import PartitionSpec as P

MOST = 8


NEG = -1e30


def body(embeddings, class_rows, cand_blocks, label_pos):
    gathered, cand_all, labels_all = (
        lax.all_gather(embeddings, "cls", axis=0, tiled=True),
        lax.all_gather(cand_blocks, "cls", axis=0, tiled=True),
        lax.all_gather(label_pos, "cls", axis=0, tiled=True),
    )
    local_blocks, block_taxa, feature_width = class_rows.shape
    group_lists = cand_all.shape[0]
    dp_images = gathered.shape[0]
    group_rows = dp_images // group_lists
    my_shard = lax.axis_index("cls")
    owned_ids = my_shard * local_blocks + jnp.arange(local_blocks, dtype=jnp.int32)
    matches = (cand_all[:, :, None] == owned_ids[None, None, :]).astype(jnp.int32)
    hit_count = jnp.sum(matches, axis=1)
    slot_of = jnp.sum(
        matches * jnp.arange(cand_all.shape[1], dtype=jnp.int32)[None, :, None], axis=1
    )
    hit_rank = jnp.cumsum(hit_count, axis=0) - 1
    slot_ids = jnp.arange(MOST, dtype=jnp.int32)
    picked = (
        (hit_count[:, :, None] > 0) & (hit_rank[:, :, None] == slot_ids[None, None, :])
    ).astype(jnp.int32)
    block_index = jnp.arange(group_lists, dtype=jnp.int32)[:, None, None]
    src_block = jnp.sum(picked * block_index, axis=0)
    valid_slot = jnp.sum(picked, axis=0)
    src_slot = jnp.sum(picked * slot_of[:, :, None], axis=0)
    image_tiles = gathered.reshape(group_lists, group_rows, feature_width)[src_block]
    label_tiles = labels_all.reshape(group_lists, group_rows)[src_block]
    scores = jnp.einsum(
        "jsid,jtd->jsit", image_tiles, class_rows, preferred_element_type=jnp.float32
    )
    live_slot = (valid_slot > 0)[:, :, None, None]
    target_pos = (
        src_slot[:, :, None, None] * block_taxa
        + jnp.arange(block_taxa, dtype=jnp.int32)[None, None, None, :]
    )
    is_true = (label_tiles[:, :, :, None] == target_pos) & live_slot
    true_slot = jnp.sum(jnp.where(is_true, scores, 0.0), axis=3)
    slot_max = jnp.max(scores, axis=3)
    owner_map = picked.reshape(group_lists, local_blocks * MOST)
    owner_float = owner_map.astype(jnp.float32)
    flat_max = slot_max.reshape(local_blocks * MOST, group_rows)
    local_max = jnp.max(jnp.where(owner_map[:, :, None] > 0, flat_max[None, :, :], NEG), axis=1)
    local_true = jnp.einsum(
        "bq,qi->bi", owner_float, true_slot.reshape(-1, group_rows), precision=lax.Precision.HIGHEST
    )
    score_max = lax.pmax(local_max.astype(jnp.bfloat16), "cls").astype(local_max.dtype)
    per_slot = score_max[src_block]
    exp_weights = jnp.where(live_slot, jnp.exp(scores - per_slot[:, :, :, None]), 0.0)
    exp_total, true_total = lax.psum(
        (
            jnp.einsum(
                "bq,qi->bi",
                owner_float,
                jnp.sum(exp_weights, axis=3).reshape(-1, group_rows),
                precision=lax.Precision.HIGHEST,
            ),
            local_true,
        ),
        "cls",
    )
    log_norm = score_max + jnp.log(exp_total)
    image_loss = (log_norm - true_total).reshape(dp_images)
    softmax_prob = jnp.exp(scores - log_norm[src_block][:, :, :, None])
    logit_grad = jnp.where(live_slot, softmax_prob - is_true.astype(jnp.float32), 0.0).astype(
        jnp.bfloat16
    )
    row_share = block_taxa // lax.axis_size("dp")
    whole_sum = lax.psum(
        jnp.einsum("jsit,jsid->tjd", logit_grad, image_tiles, preferred_element_type=jnp.float32),
        "dp",
    )
    class_grad = lax.dynamic_slice_in_dim(whole_sum, lax.axis_index("dp") * row_share, row_share, 0)
    return (image_loss, class_grad)


def solution(mesh):
    in_specs = (
        P(("dp", "cls"), None),
        P("cls", None, None),
        P(("dp", "cls"), None),
        P(("dp", "cls")),
    )
    out_specs = (P("dp"), P("dp", "cls", None))
    return jax.shard_map(body, mesh=mesh, in_specs=in_specs, out_specs=out_specs, check_vma=False)
```

profile of v0, /device:TPU:1, one launch (start us, length us, event | category | flops | bytes accessed | tf_op | source)
XLA Modules:
  0.0 591.8 jit_solution(9255299646218935432)
XLA Ops:
  7.2 0.7 all-gather.4.cloned.1.call-update
  8.0 33.4 %all-gather = s32[32,2,8]{2,1,0:T(2,128)S(1)} all-gather(s32[1,2,8]{2,1,0:T(2,128)} %bitcast.56), channel_id=1, replica_groups=mesh['dp'=16,'cls'=32] {'cls'}, dimensions={0}, use_global_device_ids=true | all-gather | bytes 2112 | tf_op jit(solution)/shard_map/all_gather | solution.py:15
  41.4 0.1 copy.26
  41.4 0.1 fusion.10
  41.5 0.1 copy.27
  41.6 0.1 reduce_window_sum.11
  41.7 0.1 copy.28
  41.8 0.3 select_reduce_fusion.3
  42.1 0.1 reshape.114
  42.2 0.1 eq.63
  42.3 0.1 convert_compare_fusion
  42.4 0.1 copy.29
  42.5 30.6 %all-gather.1 = s32[32,1,256]{2,1,0:T(1,128)S(1)} all-gather(s32[1,1,256]{2,1,0:T(1,128)} %bitcast.57), channel_id=1, replica_groups=mesh['dp'=16,'cls'=32] {'cls'}, dimensions={0}, use_global_device_ids=true | all-gather | bytes 33792 | tf_op jit(solution)/shard_map/all_gather | solution.py:16
  73.1 0.6 gather_fusion.2
  73.7 0.1 iota_add_fusion
  73.8 66.1 %all-gather.4.cloned.1.call-done = bf16[8192,768]{1,0:T(8,128)(2,1)} async-done(((bf16[256,768]{1,0:T(8,128)(2,1)}), bf16[8192,768]{1,0:T(8,128)(2,1)}) %all-gather.4.cloned.1.call-update) | async-done | bytes 12582928 | tf_op jit(solution)/shard_map/all_gather | solution.py:14
  139.9 8.1 %gather_fusion = bf16[32,128,768]{2,1,0:T(8,128)(2,1)} fusion(bf16[64,128,768]{2,1,0:T(8,128)(2,1)} %bitcast.48, s32[1024]{0:T(1024)S(1)} %pad_clamp_fusion), kind=kCustom, calls=%fused_computation | custom fusion | bytes 12583040 | tf_op jit(solution)/shard_map/gather | solution.py:38
  148.1 6.5 %fusion.20 = (bf16[4,8,128]{2,1,0:T(8,128)(2,1)S(1)}, f32[4,8,128,256]{3,2,1,0:T(8,128)}) fusion(bf16[4,8,128,768]{3,2,1,0:T(8,128)(2,1)} %bitcast.46, bf16[4,256,768]{2,1,0:T(8,128)(2,1)S(1)} %copy-done), kind=kOutput, calls=%fused_computation.49 | convolution fusion | flops 1611657216 | bytes 12066816 | tf_op jit(solution)/shard_map/jsid,jtd->jsit/dot_general | solution.py:40
  154.6 0.4 select_reduce_fusion.2
  155.0 111.6 %pmax.7 = bf16[64,128]{1,0:T(8,128)(2,1)S(1)} all-reduce(bf16[64,128]{1,0:T(8,128)(2,1)S(1)} %select_reduce_fusion.2), channel_id=1, replica_groups=mesh['dp'=16,'cls'=32] {'cls'}, use_global_device_ids=true, to_apply=%region_5.6 | all-reduce | flops 8192 | bytes 32768 | tf_op jit(solution)/shard_map/pmax | solution.py:58
  266.6 0.6 gather_fusion.1
  267.2 5.0 select_reduce_fusion
  272.2 0.9 convolution_bitcast_fusion
  273.0 0.9 convolution_bitcast_fusion.1
  273.9 0.0 all-reduce.4.cloned.1.call-start
  273.9 170.9 %all-reduce.6.cloned.1.call-done = (f32[64,128]{1,0:T(8,128)}, f32[64,128]{1,0:T(8,128)}) async-done(((f32[64,128]{1,0:T(8,128)}, f32[64,128]{1,0:T(8,128)}), (f32[64,128]{1,0:T(8,128)}, f32[64,128]{1,0:T(8,128)})) %all-reduce.6.cloned.1.call-update) | async-done | bytes 65552 | tf_op jit(solution)/shard_map/psum | solution.py:61
  444.9 1.4 subtract_bitcast_fusion
  446.3 0.6 gather_fusion.3
  446.9 7.6 %fusion.6 = f32[256,4,768]{0,2,1:T(8,128)} fusion(bf16[4,8,128,768]{3,2,1,0:T(8,128)(2,1)} %bitcast.47, f32[4,8,128,256]{3,2,1,0:T(8,128)} %get-tuple-element.22, f32[4,8,128]{2,1,0:T(8,128)S(1)} %bitcast.54, s32[4,8,256]{2,1,0:T(8,128)S(1)} %iota_add_fusion, s32[4,8,128]{2,1,0:T(8,128)S(1)} %bitcast.52, pred[4,8]{1,0:T(4,128)(4,1)S(1)} %broadcast_compare_fusion), kind=kOutput, calls=%fused_computation.14 | convolution fusion | flops 1617952768 | bytes 13697056 | tf_op jit(solution)/shard_map/jsit,jsid->tjd/dot_general | solution.py:81
  454.5 127.7 %all-reduce.4.cloned.1.call-done = f32[256,4,768]{0,2,1:T(8,128)} async-done(((f32[256,4,768]{0,2,1:T(8,128)}), f32[256,4,768]{0,2,1:T(8,128)}) %all-reduce.4.cloned.1.call-update) | async-done | bytes 3145744 | tf_op jit(solution)/shard_map/psum | solution.py:80
  582.2 1.9 constant_dynamic-slice_fusion
  584.1 1.1 copy.32
  (15 shorter events, 0.2 us)
Async XLA Ops:
  7.2 140.9 %copy-start = (bf16[4,256,768]{2,1,0:T(8,128)(2,1)S(1)}, bf16[4,256,768]{2,1,0:T(8,128)(2,1)}, u32[]{:S(2)}) copy-start(bf16[4,256,768]{2,1,0:T(8,128)(2,1)} %param.5) | copy-start | bytes 4718596
  7.2 132.8 %all-gather.4.cloned.1.call-start = ((), (), s32[]{:S(2)}) async-start(), calls=%async_computation | async-start | bytes 12976128 | tf_op jit(solution)/shard_map/all_gather | solution.py:14
  7.9 437.0 %all-reduce.6.cloned.1.call-start = ((), (), s32[]{:S(2)}) async-start(), calls=%async_computation.2 | async-start | bytes 131072 | tf_op jit(solution)/shard_map/psum | solution.py:61
  273.9 308.3 %all-reduce.4.cloned.1.call-start = ((), (), s32[]{:S(2)}) async-start(), calls=%async_computation.1 | async-start | bytes 6291456 | tf_op jit(solution)/shard_map/psum | solution.py:80
Sparse Core Ops, SparseCore 0:
  11.1 128.7 all-gather.3
  274.0 170.8 all-reduce.5
  454.6 127.5 all-reduce.3
where the time goes:
time: 592 us
  waiting for transfers between devices  366 us (62%)
  blocking collectives  176 us (30%)
  matrix products  15.9 us (3%)
  between operations  13.8 us (2%)
  local copies, waits for them, and re-layouts  13.4 us (2%)
  other arithmetic  7.47 us (1%)
    psum x1, waiting for transfers between devices, body(): lax.psum((jnp.einsum('bq,qi->bi', owner_float, jnp.sum(exp_weights, axis=...  171 us
    psum x1, waiting for transfers between devices, body(): lax.psum(jnp.einsum('jsit,jsid->tjd', logit_grad, image_tiles, preferred_...  128 us
    pmax x1, blocking collectives, body(): lax.pmax(local_max.astype(jnp.bfloat16), 'cls').astype(local_max.dtype)  112 us
    all_gather x1, waiting for transfers between devices, body(): lax.all_gather(embeddings, 'cls', axis=0, tiled=True)  66.1 us
    all_gather x1, blocking collectives, body(): lax.all_gather(cand_blocks, 'cls', axis=0, tiled=True)  33.4 us
    all_gather x1, blocking collectives, body(): lax.all_gather(label_pos, 'cls', axis=0, tiled=True)  30.6 us
  transfers between devices with their start and end apart: 3, of which 3 were waited for; matrix products, arithmetic and copies ran while one was open for 0% of the time, Pallas kernels for 0%

commit v1 on v0

--- a/solution.py
+++ b/solution.py
@@ -1,12 +1,97 @@
 import jax
 import jax.numpy as jnp
 from jax import lax
+from jax.experimental import pallas as pl
+from jax.experimental.pallas import tpu as pltpu
 from jax.sharding import PartitionSpec as P
 
 MOST = 8
+NEG = -3.0e38
+N_CLS = 32
 
 
-NEG = -1e30
+def stats_kernel(stats_ref, out_ref, recv, mine, send_a, recv_a, send_b, recv_b):
+    me = lax.axis_index("cls")
+    barrier = pltpu.get_barrier_semaphore()
+
+    def greet(step, carry):
+        pl.semaphore_signal(barrier, inc=1, device_id={"cls": (me + step) % N_CLS})
+        return carry
+
+    lax.fori_loop(1, N_CLS, greet, 0)
+    pl.semaphore_wait(barrier, N_CLS - 1)
+
+    def part_copy(step):
+        target = (me + step) % N_CLS
+        return pltpu.make_async_remote_copy(
+            src_ref=stats_ref.at[target],
+            dst_ref=recv.at[step],
+            send_sem=send_a.at[step],
+            recv_sem=recv_a.at[step],
+            device_id={"cls": target},
+        )
+
+    def start_part(step, carry):
+        part_copy(step).start()
+        return carry
+
+    def wait_part(step, carry):
+        part_copy(step).wait()
+        return carry
+
+    lax.fori_loop(1, N_CLS, start_part, 0)
+    recv[0] = stats_ref[me]
+    lax.fori_loop(1, N_CLS, wait_part, 0)
+
+    parts = recv[...]
+    tops = parts[:, 0:2, :]
+    top = jnp.max(tops, axis=0)
+    total = jnp.sum(jnp.exp(tops - top[None]) * parts[:, 2:4, :], axis=0)
+    true_score = jnp.sum(parts[:, 4:6, :], axis=0)
+    log_norm = top + jnp.log(total)
+    mine[0:2, :] = log_norm
+    mine[2:4, :] = log_norm - true_score
+    mine[4:8, :] = jnp.zeros((4, 128), jnp.float32)
+    out_ref[me] = mine[...]
+
+    def whole_copy(step):
+        return pltpu.make_async_remote_copy(
+            src_ref=mine,
+            dst_ref=out_ref.at[me],
+            send_sem=send_b.at[step],
+            recv_sem=recv_b.at[step],
+            device_id={"cls": (me + step) % N_CLS},
+        )
+
+    def start_whole(step, carry):
+        whole_copy(step).start()
+        return carry
+
+    def wait_whole(step, carry):
+        whole_copy(step).wait()
+        return carry
+
+    lax.fori_loop(1, N_CLS, start_whole, 0)
+    lax.fori_loop(1, N_CLS, wait_whole, 0)
+
+
+def combine_stats(stats):
+    return pl.pallas_call(
+        stats_kernel,
+        out_shape=jax.ShapeDtypeStruct((N_CLS, 8, 128), jnp.float32),
+        in_specs=[pl.BlockSpec(memory_space=pltpu.VMEM)],
+        out_specs=pl.BlockSpec(memory_space=pltpu.VMEM),
+        scratch_shapes=[
+            pltpu.VMEM((N_CLS, 8, 128), jnp.float32),
+            pltpu.VMEM((8, 128), jnp.float32),
+            pltpu.SemaphoreType.DMA((N_CLS,)),
+            pltpu.SemaphoreType.DMA((N_CLS,)),
+            pltpu.SemaphoreType.DMA((N_CLS,)),
+            pltpu.SemaphoreType.DMA((N_CLS,)),
+        ],
+        compiler_params=pltpu.CompilerParams(collective_id=0, has_side_effects=True),
+        name="stats_combine",
+    )(stats)
 
 
 def body(embeddings, class_rows, cand_blocks, label_pos):
@@ -46,42 +131,42 @@
         + jnp.arange(block_taxa, dtype=jnp.int32)[None, None, None, :]
     )
     is_true = (label_tiles[:, :, :, None] == target_pos) & live_slot
-    true_slot = jnp.sum(jnp.where(is_true, scores, 0.0), axis=3)
+    slot_true = jnp.sum(jnp.where(is_true, scores, 0.0), axis=3)
     slot_max = jnp.max(scores, axis=3)
+    slot_sum = jnp.sum(jnp.exp(scores - slot_max[..., None]), axis=3)
     owner_map = picked.reshape(group_lists, local_blocks * MOST)
     owner_float = owner_map.astype(jnp.float32)
     flat_max = slot_max.reshape(local_blocks * MOST, group_rows)
     local_max = jnp.max(jnp.where(owner_map[:, :, None] > 0, flat_max[None, :, :], NEG), axis=1)
-    local_true = jnp.einsum(
-        "bq,qi->bi", owner_float, true_slot.reshape(-1, group_rows), precision=lax.Precision.HIGHEST
+    base = local_max[src_block.reshape(-1)]
+    scaled = jnp.where(
+        valid_slot.reshape(-1, 1) > 0,
+        jnp.exp(flat_max - base) * slot_sum.reshape(-1, group_rows),
+        0.0,
     )
-    score_max = lax.pmax(local_max.astype(jnp.bfloat16), "cls").astype(local_max.dtype)
-    per_slot = score_max[src_block]
-    exp_weights = jnp.where(live_slot, jnp.exp(scores - per_slot[:, :, :, None]), 0.0)
-    exp_total, true_total = lax.psum(
-        (
-            jnp.einsum(
-                "bq,qi->bi",
-                owner_float,
-                jnp.sum(exp_weights, axis=3).reshape(-1, group_rows),
-                precision=lax.Precision.HIGHEST,
-            ),
-            local_true,
-        ),
-        "cls",
+    sums = jnp.einsum(
+        "bq,qi->bi",
+        owner_float,
+        jnp.concatenate([scaled, slot_true.reshape(-1, group_rows)], axis=1),
+        precision=lax.Precision.HIGHEST,
     )
-    log_norm = score_max + jnp.log(exp_total)
-    image_loss = (log_norm - true_total).reshape(dp_images)
+    local_sum, local_true = sums[:, :group_rows], sums[:, group_rows:]
+    per = group_lists // N_CLS
+    parts = [a.reshape(N_CLS, per, group_rows) for a in (local_max, local_sum, local_true)]
+    parts.append(jnp.zeros((N_CLS, 8 - 3 * per, group_rows), jnp.float32))
+    combined = combine_stats(jnp.concatenate(parts, axis=1))
+    log_norm = combined[:, 0:per].reshape(group_lists, group_rows)
+    image_loss = combined[:, per : 2 * per].reshape(dp_images)
     softmax_prob = jnp.exp(scores - log_norm[src_block][:, :, :, None])
     logit_grad = jnp.where(live_slot, softmax_prob - is_true.astype(jnp.float32), 0.0).astype(
         jnp.bfloat16
     )
-    row_share = block_taxa // lax.axis_size("dp")
-    whole_sum = lax.psum(
+    class_grad = lax.psum_scatter(
         jnp.einsum("jsit,jsid->tjd", logit_grad, image_tiles, preferred_element_type=jnp.float32),
         "dp",
+        scatter_dimension=0,
+        tiled=True,
     )
-    class_grad = lax.dynamic_slice_in_dim(whole_sum, lax.axis_index("dp") * row_share, row_share, 0)
     return (image_loss, class_grad)
 
 

time: 592 us -> 329 us (0.56)
  waiting for transfers between devices: 366 us -> 190 us
  blocking collectives: 176 us -> 64.1 us
  Pallas kernels: 0 us -> 18.9 us
  local copies, waits for them, and re-layouts: 13.4 us -> 20.1 us
    psum x2 -> x0, waiting for transfers between devices: 299 us -> none  [the longest x1 171 us: body(): lax.psum((jnp.einsum('bq,qi->bi', owner_float, jnp.sum(exp_weights, axis=...]
    unnamed x3, waiting for transfers between devices: 0.71 us -> 124 us
    pmax x1 -> x0, blocking collectives: 112 us -> none  [body(): lax.pmax(local_max.astype(jnp.bfloat16), 'cls').astype(local_max.dtype)]
    pallas_call x0 -> x1, Pallas kernels: none -> 18.9 us  [combine_stats(): pl.pallas_call(stats_kernel, out_shape=jax.ShapeDtypeStruct((N_CLS, 8, 12...]
  transfers between devices with their start and end apart: 3 -> 2, of which waited for: 3 -> 2; matrix products, arithmetic and copies ran while one was open for 0% -> 1% of each run, Pallas kernels for 0% -> 0%
where the time goes in v1:
time: 329 us
  waiting for transfers between devices  190 us (58%)
  blocking collectives  64.1 us (19%)
  local copies, waits for them, and re-layouts  20.1 us (6%)
  Pallas kernels  18.9 us (6%)
  between operations  14.8 us (4%)
  matrix products  14.5 us (4%)
  other arithmetic  6.78 us (2%)
    unnamed x3, waiting for transfers between devices  124 us
    all_gather x1, waiting for transfers between devices, body(): lax.all_gather(embeddings, 'cls', axis=0, tiled=True)  65.8 us
    all_gather x1, blocking collectives, body(): lax.all_gather(cand_blocks, 'cls', axis=0, tiled=True)  33.4 us
    all_gather x1, blocking collectives, body(): lax.all_gather(label_pos, 'cls', axis=0, tiled=True)  30.7 us
    pallas_call x1, Pallas kernels, combine_stats(): pl.pallas_call(stats_kernel, out_shape=jax.ShapeDtypeStruct((N_CLS, 8, 12...  18.9 us
    gather x1, local copies, waits for them, and re-layouts, body(): gathered.reshape(group_lists, group_rows, feature_width)[src_block]  8.14 us
    dot_general x1, matrix products, body(): jnp.einsum('jsit,jsid->tjd', logit_grad, image_tiles, preferred_element_t...  7.64 us
  transfers between devices with their start and end apart: 2, of which 2 were waited for; matrix products, arithmetic and copies ran while one was open for 1% of the time, Pallas kernels for 0%

profile of v1, /device:TPU:1, one launch (start us, length us, event | category | flops | bytes accessed | tf_op | source)
XLA Modules:
  0.0 328.8 jit_solution(10877003199613472917)
XLA Ops:
  7.2 0.7 all-gather.4.cloned.1.call-update
  8.0 33.4 %all-gather = s32[32,2,8]{2,1,0:T(2,128)S(1)} all-gather(s32[1,2,8]{2,1,0:T(2,128)} %bitcast.74), channel_id=1, replica_groups=mesh['dp'=16,'cls'=32] {'cls'}, dimensions={0}, use_global_device_ids=true | all-gather | bytes 2112 | tf_op jit(solution)/shard_map/all_gather | solution.py:100
  41.4 0.1 fusion.14
  41.5 0.1 copy.22
  41.6 0.1 reduce_window_sum.11
  41.8 0.3 convert_reduce_fusion
  42.1 0.1 reshape.157
  42.2 0.1 reshape.167
  42.3 0.1 eq.61
  42.4 0.1 convert_compare_fusion
  42.5 0.1 copy.24
  42.6 0.1 gt.49
  42.7 30.7 %all-gather.1 = s32[32,1,256]{2,1,0:T(1,128)S(1)} all-gather(s32[1,1,256]{2,1,0:T(1,128)} %bitcast.75), channel_id=1, replica_groups=mesh['dp'=16,'cls'=32] {'cls'}, dimensions={0}, use_global_device_ids=true | all-gather | bytes 33792 | tf_op jit(solution)/shard_map/all_gather | solution.py:101
  73.4 0.6 gather_fusion.2
  73.9 0.1 pad.3.clone
  74.0 0.1 iota_add_fusion
  74.1 65.8 %all-gather.4.cloned.1.call-done = bf16[8192,768]{1,0:T(8,128)(2,1)} async-done(((bf16[256,768]{1,0:T(8,128)(2,1)}), bf16[8192,768]{1,0:T(8,128)(2,1)}) %all-gather.4.cloned.1.call-update) | async-done | bytes 12582928 | tf_op jit(solution)/shard_map/all_gather | solution.py:99
  139.9 8.1 %gather_fusion = bf16[32,128,768]{2,1,0:T(8,128)(2,1)} fusion(bf16[64,128,768]{2,1,0:T(8,128)(2,1)} %bitcast.61, s32[1024]{0:T(1024)S(1)} %pad_clamp_fusion.1), kind=kCustom, calls=%fused_computation | custom fusion | bytes 12583040 | tf_op jit(solution)/shard_map/gather | solution.py:123
  148.1 6.5 %fusion.27 = (f32[4,8,128]{2,1,0:T(8,128)S(1)}, f32[4,8,128,256]{3,2,1,0:T(8,128)}) fusion(bf16[4,8,128,768]{3,2,1,0:T(8,128)(2,1)} %bitcast.59, bf16[4,256,768]{2,1,0:T(8,128)(2,1)S(1)} %copy-done), kind=kOutput, calls=%fused_computation.57 | convolution fusion | flops 1611657216 | bytes 12075008 | tf_op jit(solution)/shard_map/jsid,jtd->jsit/dot_general | solution.py:125
  154.6 0.4 select_reduce_fusion.1
  155.0 0.6 gather_fusion.1
  155.6 4.9 %exponential_reduce_fusion = (f32[4,8,128]{2,1,0:T(8,128)S(1)}, f32[4,8,128]{2,1,0:T(8,128)S(1)}) fusion(f32[4,8,128,256]{3,2,1,0:T(8,128)} %get-tuple-element.18, f32[4,8,128]{2,1,0:T(8,128)S(1)} %get-tuple-element.17, pred[4,8]{1,0:T(4,128)(4,1)S(1)} %broadcast_compare_fusion, s32[4,8,256]{2,1,0:T(8,128)S(1)} %iota_add_fusion, s32[4,8,128]{2,1,0:T(8,128)S(1)} %bitcast.69), kind=kLoop, calls=%fused_computation.6 | loop fusion | flops 6283264 | bytes 4292640 | tf_op jit(solution)/shard_map/reduce_sum | solution.py:136
  160.5 0.3 fusion.9
  160.9 0.7 maximum_maximum_fusion.stats_ref
  161.6 18.9 %stats_combine.1 = f32[32,8,128]{2,1,0:T(8,128)} custom-call(f32[32,8,128]{2,1,0:T(8,128)} %maximum_maximum_fusion.stats_ref), custom_call_target="tpu_custom_call" | custom-call | tf_op jit(solution)/shard_map/stats_combine/pallas_call | solution.py:79
  180.5 1.6 fusion.25
  182.1 0.6 gather_fusion.3
  182.7 7.6 %fusion.6 = f32[256,4,768]{0,2,1:T(8,128)} fusion(bf16[4,8,128,768]{3,2,1,0:T(8,128)(2,1)} %bitcast.60, f32[4,8,128,256]{3,2,1,0:T(8,128)} %get-tuple-element.18, f32[4,8,128]{2,1,0:T(8,128)S(1)} %bitcast.73, s32[4,8,256]{2,1,0:T(8,128)S(1)} %iota_add_fusion, s32[4,8,128]{2,1,0:T(8,128)S(1)} %bitcast.70, pred[4,8]{1,0:T(4,128)(4,1)S(1)} %broadcast_compare_fusion), kind=kOutput, calls=%fused_computation.14 | convolution fusion | flops 1617952768 | bytes 13697056 | tf_op jit(solution)/shard_map/jsit,jsid->tjd/dot_general | solution.py:165
  190.3 5.0 %copy.27 = f32[256,4,768]{2,1,0:T(4,128)} copy(f32[256,4,768]{0,2,1:T(8,128)} %fusion.6) | data formatting | bytes 6291456 | tf_op jit(solution)/shard_map/jsit,jsid->tjd/transpose | solution.py:165
  195.3 1.3 dynamic-slice
  197.3 123.1 %all-reduce.3.cloned.1.call-done = f32[256,4,768]{2,1,0:T(4,128)} async-done(((f32[256,4,768]{2,1,0:T(4,128)}), f32[256,4,768]{2,1,0:T(4,128)}) %all-reduce.3.cloned.1.call-update) | async-done | bytes 3145744
  320.3 1.6 constant_dynamic-slice_fusion
  (20 shorter events, 0.4 us)
Async XLA Ops:
  7.2 140.9 %copy-start = (bf16[4,256,768]{2,1,0:T(8,128)(2,1)S(1)}, bf16[4,256,768]{2,1,0:T(8,128)(2,1)}, u32[]{:S(2)}) copy-start(bf16[4,256,768]{2,1,0:T(8,128)(2,1)} %param.5) | copy-start | bytes 4718596
  7.2 132.8 %all-gather.4.cloned.1.call-start = ((), (), s32[]{:S(2)}) async-start(), calls=%async_computation | async-start | bytes 12976128 | tf_op jit(solution)/shard_map/all_gather | solution.py:99
  7.9 312.4 %all-reduce.3.cloned.1.call-start = ((), (), s32[]{:S(2)}) async-start(), calls=%async_computation.1 | async-start | bytes 6291456
Sparse Core Ops, SparseCore 0:
  11.1 128.7 all-gather.3
  195.4 124.8 all-reduce.2

commit v2 on v1

--- a/solution.py
+++ b/solution.py
@@ -94,13 +94,261 @@
     )(stats)
 
 
+NX, NY, NZ = 4, 8, 8
+A_ROWS = 96
+
+
+def relay_order(rows):
+    rate = 46.0
+    rate = rate * 1000.0 / 1536.0
+    hop = 1.7
+    a_rows, b_rows = A_ROWS, rows - A_ROWS
+    free = {"x+": 0.0, "x-": 0.0, "y+": 0.0, "y-": 0.0}
+    queue, serial, order = [], 0, []
+
+    def span(kind, u, v):
+        size, start = (a_rows, 0) if kind == "A" else (b_rows, a_rows)
+        first, second = (u, v) if kind == "A" else (v, u)
+        far1, far2 = (NX // 2, NY // 2) if kind == "A" else (NY // 2, NX // 2)
+        if abs(first) == far1:
+            return (start, size // 2) if first < 0 else (start + size // 2, size // 2)
+        if abs(second) == far2:
+            return (start, size // 2) if second < 0 else (start + size // 2, size // 2)
+        return start, size
+
+    def sends(kind, u, v, came):
+        result = []
+        first_axis = "x" if kind == "A" else "y"
+        for axis in ("x", "y"):
+            pos, far = (u, NX // 2) if axis == "x" else (v, NY // 2)
+            if axis == first_axis and came is not None and came[0] != first_axis:
+                continue
+            for sign in ("+", "-"):
+                if came is not None and came[0] == axis and came[1] != sign:
+                    continue
+                new = pos - 1 if sign == "+" else pos + 1
+                if abs(new) > far:
+                    continue
+                if axis != first_axis and abs(new) == far:
+                    first, far1 = (u, NX // 2) if kind == "A" else (v, NY // 2)
+                    if abs(first) == far1 and (first < 0) != (new < 0):
+                        continue
+                result.append((axis + sign, (new, v) if axis == "x" else (u, new)))
+        result.sort(key=lambda item: item[0][0] != first_axis)
+        return result
+
+    def launch(now, kind, u, v, came):
+        nonlocal serial
+        out = []
+        for direction, (nu, nv) in sends(kind, u, v, came):
+            start, size = span(kind, nu, nv)
+            free[direction] = max(free[direction], now) + size / rate
+            queue.append((free[direction] + hop, serial, kind, nu, nv, direction))
+            serial += 1
+            out.append((direction, nu, nv, start, size))
+        return out
+
+    first = [("A", launch(0.0, "A", 0, 0, None)), ("B", launch(0.0, "B", 0, 0, None))]
+    while queue:
+        queue.sort()
+        now, _, kind, u, v, direction = queue.pop(0)
+        start, size = span(kind, u, v)
+        order.append((kind, u, v, start, size, launch(now, kind, u, v, direction)))
+    return first, order
+
+
+def gather_kernel(own_ref, small_ref, out_ref, small_out, send, recv, local, small_send, small_recv):
+    me = lax.axis_index("cls")
+    x, y = me // NY, me % NY
+    barrier = pltpu.get_barrier_semaphore()
+
+    def greet(step, carry):
+        pl.semaphore_signal(barrier, inc=1, device_id={"cls": (me + step) % N_CLS})
+        return carry
+
+    lax.fori_loop(1, N_CLS, greet, 0)
+    pl.semaphore_wait(barrier, N_CLS - 1)
+
+    rows = own_ref.shape[0]
+    first, order = relay_order(rows)
+    near = {
+        "x+": ((x + 1) % NX) * NY + y,
+        "x-": ((x + NX - 1) % NX) * NY + y,
+        "y+": x * NY + (y + 1) % NY,
+        "y-": x * NY + (y + NY - 1) % NY,
+    }
+    number = {(kind, u, v): i for i, (kind, u, v, _, _, _) in enumerate(order)}
+    sent = []
+
+    def slot_of(u, v):
+        return ((x + u + NX) % NX) * NY + (y + v + NY) % NY
+
+    def begin(kind, u, v, outs):
+        slot = slot_of(u, v)
+        for direction, nu, nv, start, size in outs:
+            index = number[(kind, nu, nv)]
+            source = own_ref if (u, v) == (0, 0) else out_ref.at[slot]
+            copy = pltpu.make_async_remote_copy(
+                src_ref=source.at[pl.ds(start, size)],
+                dst_ref=out_ref.at[slot, pl.ds(start, size)],
+                send_sem=send.at[index],
+                recv_sem=recv.at[index],
+                device_id={"cls": near[direction]},
+            )
+            copy.start()
+            sent.append(copy)
+
+    def small_copy(step):
+        return pltpu.make_async_remote_copy(
+            src_ref=small_ref,
+            dst_ref=small_out.at[me],
+            send_sem=small_send.at[step],
+            recv_sem=small_recv.at[step],
+            device_id={"cls": (me + step) % N_CLS},
+        )
+
+    def start_small(step, carry):
+        small_copy(step).start()
+        return carry
+
+    def wait_small(step, carry):
+        small_copy(step).wait()
+        return carry
+
+    for kind, outs in first:
+        begin(kind, 0, 0, outs)
+    lax.fori_loop(1, N_CLS, start_small, 0)
+    own = pltpu.make_async_copy(own_ref, out_ref.at[me], local.at[0])
+    own.start()
+    small_own = pltpu.make_async_copy(small_ref, small_out.at[me], local.at[1])
+    small_own.start()
+    for index, (kind, u, v, start, size, outs) in enumerate(order):
+        pltpu.make_async_remote_copy(
+            src_ref=own_ref.at[pl.ds(start, size)],
+            dst_ref=out_ref.at[slot_of(u, v), pl.ds(start, size)],
+            send_sem=send.at[index],
+            recv_sem=recv.at[index],
+            device_id={"cls": near["x+"]},
+        ).wait_recv()
+        begin(kind, u, v, outs)
+    lax.fori_loop(1, N_CLS, wait_small, 0)
+    own.wait()
+    small_own.wait()
+    for copy in sent:
+        copy.wait_send()
+
+
+def gather_images(embeddings, small):
+    rows, width = embeddings.shape
+    parts = len(relay_order(rows)[1])
+    return pl.pallas_call(
+        gather_kernel,
+        out_shape=[
+            jax.ShapeDtypeStruct((N_CLS, rows, width), embeddings.dtype),
+            jax.ShapeDtypeStruct((N_CLS,) + small.shape, small.dtype),
+        ],
+        in_specs=[pl.BlockSpec(memory_space=pltpu.VMEM), pl.BlockSpec(memory_space=pltpu.VMEM)],
+        out_specs=[pl.BlockSpec(memory_space=pltpu.HBM), pl.BlockSpec(memory_space=pltpu.VMEM)],
+        scratch_shapes=[
+            pltpu.SemaphoreType.DMA((parts,)),
+            pltpu.SemaphoreType.DMA((parts,)),
+            pltpu.SemaphoreType.DMA((2,)),
+            pltpu.SemaphoreType.DMA((N_CLS,)),
+            pltpu.SemaphoreType.DMA((N_CLS,)),
+        ],
+        compiler_params=pltpu.CompilerParams(collective_id=1, has_side_effects=True),
+        name="gather_images",
+    )(embeddings, small)
+
+
+def scatter_kernel(grad_ref, out_ref, pair, arrived, held, send_p, recv_p, send_r, recv_r):
+    dp = lax.axis_index("dp")
+    z, core = dp // 2, dp % 2
+    other = z * 2 + (1 - core)
+    up, down = ((z + 1) % NZ) * 2 + core, ((z + NZ - 1) % NZ) * 2 + core
+    barrier = pltpu.get_barrier_semaphore()
+    for target in (other, up, down):
+        pl.semaphore_signal(barrier, inc=1, device_id={"dp": target})
+    pl.semaphore_wait(barrier, 3)
+    chains = grad_ref.shape[0]
+
+    def chunk_of(chain, step):
+        if chain < chains // 2:
+            return (z + NZ - 1 - step) % NZ
+        return (z + 1 + step) % NZ
+
+    def pair_copy(chain, step):
+        return pltpu.make_async_remote_copy(
+            src_ref=grad_ref.at[chain, chunk_of(chain, step) * 2 + (1 - core)],
+            dst_ref=pair.at[chain, step],
+            send_sem=send_p.at[chain, step],
+            recv_sem=recv_p.at[chain, step],
+            device_id={"dp": other},
+        )
+
+    def ring_copy(chain, step):
+        return pltpu.make_async_remote_copy(
+            src_ref=held.at[chain, step],
+            dst_ref=arrived.at[chain, step],
+            send_sem=send_r.at[chain, step],
+            recv_sem=recv_r.at[chain, step],
+            device_id={"dp": up if chain < chains // 2 else down},
+        )
+
+    order = [0, chains // 2, 1, chains // 2 + 1]
+    for step in range(NZ):
+        for chain in order:
+            pair_copy(chain, step).start()
+    for step in range(NZ):
+        for chain in order:
+            pair_copy(chain, step).wait_recv()
+            value = grad_ref[chain, chunk_of(chain, step) * 2 + core] + pair[chain, step]
+            if step > 0:
+                ring_copy(chain, step - 1).wait_recv()
+                value = value + arrived[chain, step - 1]
+            if step < NZ - 1:
+                held[chain, step] = value
+                ring_copy(chain, step).start()
+            else:
+                out_ref[chain] = value
+    for step in range(NZ):
+        for chain in order:
+            pair_copy(chain, step).wait_send()
+            if step < NZ - 1:
+                ring_copy(chain, step).wait_send()
+
+
+def scatter_grad(grad):
+    chains, shares, rows, width = grad.shape
+    return pl.pallas_call(
+        scatter_kernel,
+        out_shape=jax.ShapeDtypeStruct((chains, rows, width), jnp.float32),
+        in_specs=[pl.BlockSpec(memory_space=pltpu.VMEM)],
+        out_specs=pl.BlockSpec(memory_space=pltpu.VMEM),
+        scratch_shapes=[
+            pltpu.VMEM((chains, NZ, rows, width), jnp.float32),
+            pltpu.VMEM((chains, NZ, rows, width), jnp.float32),
+            pltpu.VMEM((chains, NZ, rows, width), jnp.float32),
+            pltpu.SemaphoreType.DMA((chains, NZ)),
+            pltpu.SemaphoreType.DMA((chains, NZ)),
+            pltpu.SemaphoreType.DMA((chains, NZ)),
+            pltpu.SemaphoreType.DMA((chains, NZ)),
+        ],
+        compiler_params=pltpu.CompilerParams(collective_id=2, has_side_effects=True),
+        name="scatter_grad",
+    )(grad)
+
+
 def body(embeddings, class_rows, cand_blocks, label_pos):
-    gathered, cand_all, labels_all = (
-        lax.all_gather(embeddings, "cls", axis=0, tiled=True),
-        lax.all_gather(cand_blocks, "cls", axis=0, tiled=True),
-        lax.all_gather(label_pos, "cls", axis=0, tiled=True),
-    )
     local_blocks, block_taxa, feature_width = class_rows.shape
+    own_images, (own_lists, listed) = label_pos.shape[0], cand_blocks.shape
+    small = jnp.concatenate([label_pos, cand_blocks.reshape(-1)])
+    small = jnp.pad(small, (0, 8 * 128 - small.shape[0])).reshape(8, 128)
+    gathered, small_all = gather_images(embeddings, small)
+    gathered = gathered.reshape(N_CLS * own_images, feature_width)
+    small_all = small_all.reshape(N_CLS, 8 * 128)
+    labels_all = small_all[:, :own_images].reshape(-1)
+    cand_all = small_all[:, own_images : own_images + own_lists * listed].reshape(-1, listed)
     group_lists = cand_all.shape[0]
     dp_images = gathered.shape[0]
     group_rows = dp_images // group_lists
@@ -161,12 +409,12 @@
     logit_grad = jnp.where(live_slot, softmax_prob - is_true.astype(jnp.float32), 0.0).astype(
         jnp.bfloat16
     )
-    class_grad = lax.psum_scatter(
-        jnp.einsum("jsit,jsid->tjd", logit_grad, image_tiles, preferred_element_type=jnp.float32),
-        "dp",
-        scatter_dimension=0,
-        tiled=True,
-    )
+    grad = jnp.einsum(
+        "jsit,jsid->jtd", logit_grad, image_tiles, preferred_element_type=jnp.float32
+    )
+    shares = lax.axis_size("dp")
+    grad = grad.reshape(local_blocks, shares, block_taxa // shares, feature_width)
+    class_grad = scatter_grad(grad).transpose(1, 0, 2)
     return (image_loss, class_grad)
 
 

time: 329 us -> 183 us (0.56)
  the two profiles are of different devices: /device:TPU:1 before, /device:TPU:8 now
where the time goes in v2:
time: 183 us; the launch traced here: 182 us
  Pallas kernels  144 us (79%)
  local copies, waits for them, and re-layouts  16.5 us (9%)
  matrix products  13.6 us (7%)
  other arithmetic  7.45 us (4%)
    pallas_call x1, Pallas kernels, gather_images(): pl.pallas_call(gather_kernel, out_shape=[jax.ShapeDtypeStruct((N_CLS, row...  85 us
    pallas_call x1, Pallas kernels, scatter_grad(): pl.pallas_call(scatter_kernel, out_shape=jax.ShapeDtypeStruct((chains, ro...  38 us
    pallas_call x1, Pallas kernels, combine_stats(): pl.pallas_call(stats_kernel, out_shape=jax.ShapeDtypeStruct((N_CLS, 8, 12...  20.7 us
    gather x1, local copies, waits for them, and re-layouts, body(): gathered.reshape(group_lists, group_rows, feature_width)[src_block]  8.14 us
    dot_general x1, matrix products, body(): jnp.einsum('jsit,jsid->jtd', logit_grad, image_tiles, preferred_element_t...  6.74 us
    dot_general x1, matrix products, body(): jnp.einsum('jsid,jtd->jsit', image_tiles, class_rows, preferred_element_t...  6.54 us
    reduce_sum x1, other arithmetic, body(): slot_sum = jnp.sum(jnp.exp(scores - slot_max[..., None]), axis=3)  4.88 us

profile of v2, /device:TPU:8, one launch (start us, length us, event | category | flops | bytes accessed | tf_op | source)
XLA Modules:
  0.0 182.0 jit_solution(17808706534106059025)
XLA Ops:
  0.7 0.9 reshape.161
  1.5 0.1 pad.8.clone
  1.6 0.7 pad_add_fusion
  2.3 0.6 pad_bitcast_fusion.small_ref
  2.9 0.1 eq.64
  3.0 85.0 %gather_images.1 = (bf16[32,256,768]{2,1,0:T(8,128)(2,1)}, s32[32,8,128]{2,1,0:T(8,128)}) custom-call(bf16[256,768]{1,0:T(8,128)(2,1)} %own_ref.1, s32[8,128]{1,0:T(8,128)} %pad_bitcast_fusion.small_ref), custom_call_target="tpu_custom_call" | custom-call | tf_op jit(solution)/shard_map/gather_images/pallas_call | solution.py:244
  88.0 0.9 copy.24
  89.1 0.1 fusion.13
  89.3 0.1 copy.14
  89.4 0.1 reduce_window_sum.11
  89.5 0.1 copy.15
  89.5 0.1 convert_compare_fusion
  89.6 0.1 copy.16
  89.7 0.3 convert_reduce_fusion
  90.0 0.1 gt.49
  90.1 0.1 reshape.165
  90.2 0.1 reshape.175
  90.3 8.1 %gather_fusion = bf16[32,128,768]{2,1,0:T(8,128)(2,1)} fusion(bf16[64,128,768]{2,1,0:T(8,128)(2,1)} %bitcast.61, s32[1024]{0:T(1024)S(1)} %pad_clamp_fusion.1), kind=kCustom, calls=%fused_computation | custom fusion | bytes 12583040 | tf_op jit(solution)/shard_map/gather | solution.py:371
  98.4 0.6 gather_fusion.2
  99.0 0.1 iota_add_fusion
  99.1 6.5 %fusion.26 = (f32[4,8,128]{2,1,0:T(8,128)S(1)}, f32[4,8,128,256]{3,2,1,0:T(8,128)}) fusion(bf16[4,8,128,768]{3,2,1,0:T(8,128)(2,1)} %bitcast.58, bf16[4,256,768]{2,1,0:T(8,128)(2,1)S(1)} %copy-done), kind=kOutput, calls=%fused_computation.58 | convolution fusion | flops 1611657216 | bytes 12075008 | tf_op jit(solution)/shard_map/jsid,jtd->jsit/dot_general | solution.py:373
  105.6 0.4 select_reduce_fusion.1
  106.0 0.6 gather_fusion.1
  106.6 4.9 %exponential_reduce_fusion = (f32[4,8,128]{2,1,0:T(8,128)S(1)}, f32[4,8,128]{2,1,0:T(8,128)S(1)}) fusion(f32[4,8,128,256]{3,2,1,0:T(8,128)} %get-tuple-element.24, f32[4,8,128]{2,1,0:T(8,128)S(1)} %get-tuple-element.23, pred[4,8]{1,0:T(4,128)(4,1)S(1)} %broadcast_compare_fusion, s32[4,8,256]{2,1,0:T(8,128)S(1)} %iota_add_fusion, s32[4,8,128]{2,1,0:T(8,128)S(1)} %bitcast.71), kind=kLoop, calls=%fused_computation.6 | loop fusion | flops 6283264 | bytes 4292640 | tf_op jit(solution)/shard_map/reduce_sum | solution.py:384
  111.6 0.3 fusion.8
  111.9 0.7 maximum_maximum_fusion.stats_ref
  112.7 20.7 %stats_combine.1 = f32[32,8,128]{2,1,0:T(8,128)} custom-call(f32[32,8,128]{2,1,0:T(8,128)} %maximum_maximum_fusion.stats_ref), custom_call_target="tpu_custom_call" | custom-call | tf_op jit(solution)/shard_map/stats_combine/pallas_call | solution.py:79
  133.3 1.6 fusion.24
  134.9 0.6 gather_fusion.3
  135.5 6.7 %fusion = f32[4,256,768,1]{2,1,3,0:T(8,128)} fusion(bf16[4,8,128,768]{3,2,1,0:T(8,128)(2,1)} %bitcast.59, f32[4,8,128,256]{3,2,1,0:T(8,128)} %get-tuple-element.24, f32[4,8,128]{2,1,0:T(8,128)S(1)} %bitcast.75, s32[4,8,256]{2,1,0:T(8,128)S(1)} %iota_add_fusion, s32[4,8,128]{2,1,0:T(8,128)S(1)} %bitcast.72, pred[4,8]{1,0:T(4,128)(4,1)S(1)} %broadcast_compare_fusion), kind=kOutput, calls=%fused_computation.8 | convolution fusion | flops 1617952768 | bytes 13697056 | tf_op jit(solution)/shard_map/jsit,jsid->jtd/dot_general | solution.py:412
  142.3 38.0 %scatter_grad.1 = f32[4,16,768]{2,1,0:T(8,128)} custom-call(f32[4,16,16,768]{3,2,1,0:T(8,128)} %bitcast.60), custom_call_target="tpu_custom_call" | custom-call | tf_op jit(solution)/shard_map/scatter_grad/pallas_call | solution.py:323
  180.3 1.7 copy.18
  (20 shorter events, 0.3 us)
Async XLA Ops:
  0.6 98.5 %copy-start = (bf16[4,256,768]{2,1,0:T(8,128)(2,1)S(1)}, bf16[4,256,768]{2,1,0:T(8,128)(2,1)}, u32[]{:S(2)}) copy-start(bf16[4,256,768]{2,1,0:T(8,128)(2,1)} %param.5) | copy-start | bytes 4718596

commit v3 on v2

v3 whole, which is shorter than its diff:
```python
import jax
import jax.numpy as jnp
from jax import lax
from jax.experimental import pallas as pl
from jax.experimental.pallas import tpu as pltpu
from jax.sharding import PartitionSpec as P

MOST = 8
NEG = -3.0e38
N_CLS = 32


NX, NY, NZ = 4, 8, 8
A_ROWS = 96
BLOCKS = 4


def relay_order(rows):
    rate = 30.0
    hop = 1.7
    a_rows, b_rows = A_ROWS, rows - A_ROWS
    free = {"x+": 0.0, "x-": 0.0, "y+": 0.0, "y-": 0.0}
    queue, serial, order = [], 0, []

    def span(kind, u, v):
        size, start = (a_rows, 0) if kind == "A" else (b_rows, a_rows)
        first, second = (u, v) if kind == "A" else (v, u)
        far1, far2 = (NX // 2, NY // 2) if kind == "A" else (NY // 2, NX // 2)
        if abs(first) == far1:
            return (start, size // 2) if first < 0 else (start + size // 2, size // 2)
        if abs(second) == far2:
            return (start, size // 2) if second < 0 else (start + size // 2, size // 2)
        return start, size

    def sends(kind, u, v, came):
        result = []
        first_axis = "x" if kind == "A" else "y"
        for axis in ("x", "y"):
            pos, far = (u, NX // 2) if axis == "x" else (v, NY // 2)
            if axis == first_axis and came is not None and came[0] != first_axis:
                continue
            for sign in ("+", "-"):
                if came is not None and came[0] == axis and came[1] != sign:
                    continue
                new = pos - 1 if sign == "+" else pos + 1
                if abs(new) > far:
                    continue
                if axis != first_axis and abs(new) == far:
                    first, far1 = (u, NX // 2) if kind == "A" else (v, NY // 2)
                    if abs(first) == far1 and (first < 0) != (new < 0):
                        continue
                result.append((axis + sign, (new, v) if axis == "x" else (u, new)))
        result.sort(key=lambda item: item[0][0] != first_axis)
        return result

    def launch(now, kind, u, v, came):
        nonlocal serial
        out = []
        for direction, (nu, nv) in sends(kind, u, v, came):
            start, size = span(kind, nu, nv)
            free[direction] = max(free[direction], now) + size / rate
            queue.append((free[direction] + hop, serial, kind, nu, nv, direction))
            serial += 1
            out.append((direction, nu, nv, start, size))
        return out

    first = [("A", launch(0.0, "A", 0, 0, None)), ("B", launch(0.0, "B", 0, 0, None))]
    while queue:
        queue.sort()
        now, _, kind, u, v, direction = queue.pop(0)
        start, size = span(kind, u, v)
        order.append((kind, u, v, start, size, launch(now, kind, u, v, direction)))
    return first, order


def gather_kernel(own_ref, small_ref, out_ref, small_out, send, recv, local, small_send, small_recv):
    me = lax.axis_index("cls")
    x, y = me // NY, me % NY
    barrier = pltpu.get_barrier_semaphore()

    def greet(step, carry):
        pl.semaphore_signal(barrier, inc=1, device_id={"cls": (me + step) % N_CLS})
        return carry

    lax.fori_loop(1, N_CLS, greet, 0)
    pl.semaphore_wait(barrier, N_CLS - 1)

    rows = own_ref.shape[0]
    first, order = relay_order(rows)
    near = {
        "x+": ((x + 1) % NX) * NY + y,
        "x-": ((x + NX - 1) % NX) * NY + y,
        "y+": x * NY + (y + 1) % NY,
        "y-": x * NY + (y + NY - 1) % NY,
    }
    number = {(kind, u, v): i for i, (kind, u, v, _, _, _) in enumerate(order)}
    sent = []

    def slot_of(u, v):
        return ((x + u + NX) % NX) * NY + (y + v + NY) % NY

    def begin(kind, u, v, outs):
        slot = slot_of(u, v)
        for direction, nu, nv, start, size in outs:
            index = number[(kind, nu, nv)]
            source = own_ref if (u, v) == (0, 0) else out_ref.at[slot]
            copy = pltpu.make_async_remote_copy(
                src_ref=source.at[pl.ds(start, size)],
                dst_ref=out_ref.at[slot, pl.ds(start, size)],
                send_sem=send.at[index],
                recv_sem=recv.at[index],
                device_id={"cls": near[direction]},
            )
            copy.start()
            sent.append(copy)

    def small_copy(step):
        return pltpu.make_async_remote_copy(
            src_ref=small_ref,
            dst_ref=small_out.at[me],
            send_sem=small_send.at[step],
            recv_sem=small_recv.at[step],
            device_id={"cls": (me + step) % N_CLS},
        )

    def start_small(step, carry):
        small_copy(step).start()
        return carry

    def wait_small(step, carry):
        small_copy(step).wait()
        return carry

    for kind, outs in first:
        begin(kind, 0, 0, outs)
    lax.fori_loop(1, N_CLS, start_small, 0)
    own = pltpu.make_async_copy(own_ref, out_ref.at[me], local.at[0])
    own.start()
    small_own = pltpu.make_async_copy(small_ref, small_out.at[me], local.at[1])
    small_own.start()
    for index, (kind, u, v, start, size, outs) in enumerate(order):
        pltpu.make_async_remote_copy(
            src_ref=own_ref.at[pl.ds(start, size)],
            dst_ref=out_ref.at[slot_of(u, v), pl.ds(start, size)],
            send_sem=send.at[index],
            recv_sem=recv.at[index],
            device_id={"cls": near["x+"]},
        ).wait_recv()
        begin(kind, u, v, outs)
    lax.fori_loop(1, N_CLS, wait_small, 0)
    own.wait()
    small_own.wait()
    for copy in sent:
        copy.wait_send()


def gather_images(embeddings, small):
    rows, width = embeddings.shape
    parts = len(relay_order(rows)[1])
    return pl.pallas_call(
        gather_kernel,
        out_shape=[
            jax.ShapeDtypeStruct((N_CLS, rows, width), embeddings.dtype),
            jax.ShapeDtypeStruct((N_CLS,) + small.shape, small.dtype),
        ],
        in_specs=[pl.BlockSpec(memory_space=pltpu.VMEM), pl.BlockSpec(memory_space=pltpu.VMEM)],
        out_specs=[pl.BlockSpec(memory_space=pltpu.HBM), pl.BlockSpec(memory_space=pltpu.VMEM)],
        scratch_shapes=[
            pltpu.SemaphoreType.DMA((parts,)),
            pltpu.SemaphoreType.DMA((parts,)),
            pltpu.SemaphoreType.DMA((2,)),
            pltpu.SemaphoreType.DMA((N_CLS,)),
            pltpu.SemaphoreType.DMA((N_CLS,)),
        ],
        compiler_params=pltpu.CompilerParams(collective_id=1, has_side_effects=True),
        name="gather_images",
    )(embeddings, small)


def score_kernel(src_ref, one_ref, two_ref, rows_ref, target_ref, pick_ref, scores_ref, picked_ref, stats_ref, slot_stats):
    del src_ref
    p = pl.program_id(0)
    picked_ref[0] = one_ref[0]
    picked_ref[1] = two_ref[0]
    both = jnp.concatenate([one_ref[0], two_ref[0]], axis=0)
    score = lax.dot_general(
        rows_ref[0], both, (((1,), (1,)), ((), ())), preferred_element_type=jnp.float32
    )
    taxon = lax.broadcasted_iota(jnp.int32, (256, 128), 0)
    for i in range(2):
        part = score[:, i * 128 : (i + 1) * 128]
        scores_ref[i] = part
        top = jnp.max(part, axis=0, keepdims=True)
        q = 2 * p + i
        slot_stats[q, 0:1, :] = top
        slot_stats[q, 1:2, :] = jnp.sum(jnp.exp(part - top), axis=0, keepdims=True)
        slot_stats[q, 2:3, :] = jnp.sum(
            jnp.where(taxon == target_ref[i], part, 0.0), axis=0, keepdims=True
        )

    @pl.when(p == BLOCKS * MOST // 2 - 1)
    def merge():
        list_of = lax.broadcasted_iota(jnp.int32, (2 * N_CLS, 128), 0)

        def merge_top(q, top):
            return jnp.where(list_of == pick_ref[q], jnp.maximum(top, slot_stats[q, 0:1, :]), top)

        local_top = lax.fori_loop(
            0, BLOCKS * MOST, merge_top, jnp.full((2 * N_CLS, 128), NEG, jnp.float32), unroll=4
        )

        def merge_sum(q, carry):
            total, true_score = carry
            sel = list_of == pick_ref[q]
            scaled = jnp.exp(slot_stats[q, 0:1, :] - local_top) * slot_stats[q, 1:2, :]
            return (
                total + jnp.where(sel, scaled, 0.0),
                true_score + jnp.where(sel, slot_stats[q, 2:3, :], 0.0),
            )

        zero = jnp.zeros((2 * N_CLS, 128), jnp.float32)
        local_sum, local_true = lax.fori_loop(0, BLOCKS * MOST, merge_sum, (zero, zero), unroll=4)
        for d in range(N_CLS):
            for i, array in enumerate((local_top, local_sum, local_true)):
                stats_ref[d, 2 * i : 2 * i + 2, :] = array[2 * d : 2 * d + 2, :]
            stats_ref[d, 6:8, :] = jnp.zeros((2, 128), jnp.float32)


def score_slots(src, images, class_rows, target, pick):
    slots = BLOCKS * MOST
    _, taxa, width = class_rows.shape
    return pl.pallas_call(
        score_kernel,
        grid_spec=pltpu.PrefetchScalarGridSpec(
            num_scalar_prefetch=1,
            grid=(slots // 2,),
            in_specs=[
                pl.BlockSpec((1, 128, width), lambda p, src: (src[2 * p], 0, 0)),
                pl.BlockSpec((1, 128, width), lambda p, src: (src[2 * p + 1], 0, 0)),
                pl.BlockSpec((1, taxa, width), lambda p, src: (p // (MOST // 2), 0, 0)),
                pl.BlockSpec((2, 1, 128), lambda p, src: (p, 0, 0)),
                pl.BlockSpec((slots, 1, 128), lambda p, src: (0, 0, 0)),
            ],
            out_specs=[
                pl.BlockSpec((2, taxa, 128), lambda p, src: (p, 0, 0)),
                pl.BlockSpec((2, 128, width), lambda p, src: (p, 0, 0)),
                pl.BlockSpec((N_CLS, 8, 128), lambda p, src: (0, 0, 0)),
            ],
            scratch_shapes=[pltpu.VMEM((slots, 8, 128), jnp.float32)],
        ),
        out_shape=[
            jax.ShapeDtypeStruct((slots, taxa, 128), jnp.float32),
            jax.ShapeDtypeStruct((slots, 128, width), jnp.bfloat16),
            jax.ShapeDtypeStruct((N_CLS, 8, 128), jnp.float32),
        ],
        name="score_slots",
    )(src, images, images, class_rows, target, pick)


def grad_kernel(
    stats, target_ref, pick_ref, scores_in, picked_in, lse_ref, out_ref,
    scores, picked, recv, mine, probs, grad, pair, arrived, held,
    send_a, recv_a, send_b, recv_b, send_p, recv_p, send_r, recv_r, local,
):
    me = lax.axis_index("cls")
    dp = lax.axis_index("dp")
    z, core = dp // 2, dp % 2
    other = z * 2 + (1 - core)
    up, down = ((z + 1) % NZ) * 2 + core, ((z + NZ - 1) % NZ) * 2 + core
    barrier = pltpu.get_barrier_semaphore()

    def greet(step, carry):
        pl.semaphore_signal(barrier, inc=1, device_id={"cls": (me + step) % N_CLS})
        return carry

    lax.fori_loop(1, N_CLS, greet, 0)
    for target in (other, up, down):
        pl.semaphore_signal(barrier, inc=1, device_id={"dp": target})
    take_scores = pltpu.make_async_copy(scores_in, scores, local.at[0])
    take_picked = pltpu.make_async_copy(picked_in, picked, local.at[1])
    take_scores.start()
    take_picked.start()
    pl.semaphore_wait(barrier, N_CLS + 2)

    def part_copy(step):
        target = (me + step) % N_CLS
        return pltpu.make_async_remote_copy(
            src_ref=stats.at[target],
            dst_ref=recv.at[step],
            send_sem=send_a.at[step],
            recv_sem=recv_a.at[step],
            device_id={"cls": target},
        )

    def start_part(step, carry):
        part_copy(step).start()
        return carry

    def wait_part(step, carry):
        part_copy(step).wait()
        return carry

    lax.fori_loop(1, N_CLS, start_part, 0)
    recv[0] = stats[me]
    lax.fori_loop(1, N_CLS, wait_part, 0)

    parts = recv[...]
    tops = parts[:, 0:2, :]
    top = jnp.max(tops, axis=0)
    total = jnp.sum(jnp.exp(tops - top[None]) * parts[:, 2:4, :], axis=0)
    true_score = jnp.sum(parts[:, 4:6, :], axis=0)
    log_norm = top + jnp.log(total)
    mine[0:2, :] = log_norm
    mine[2:4, :] = log_norm - true_score
    mine[4:8, :] = jnp.zeros((4, 128), jnp.float32)
    lse_ref[me] = mine[...]

    def whole_copy(step):
        return pltpu.make_async_remote_copy(
            src_ref=mine,
            dst_ref=lse_ref.at[me],
            send_sem=send_b.at[step],
            recv_sem=recv_b.at[step],
            device_id={"cls": (me + step) % N_CLS},
        )

    def start_whole(step, carry):
        whole_copy(step).start()
        return carry

    def wait_whole(step, carry):
        whole_copy(step).wait()
        return carry

    lax.fori_loop(1, N_CLS, start_whole, 0)
    lax.fori_loop(1, N_CLS, wait_whole, 0)

    norms = jnp.concatenate([lse_ref[d, 0:2, :] for d in range(N_CLS)], axis=0)
    list_of = lax.broadcasted_iota(jnp.int32, (2 * N_CLS, 128), 0)
    taxon = lax.broadcasted_iota(jnp.int32, (256, 128), 0)
    take_scores.wait()
    take_picked.wait()

    def chunk_of(chain, step):
        if chain < BLOCKS // 2:
            return (z + NZ - 1 - step) % NZ
        return (z + 1 + step) % NZ

    def pair_copy(chain, step):
        return pltpu.make_async_remote_copy(
            src_ref=grad.at[chain, chunk_of(chain, step) * 2 + (1 - core)],
            dst_ref=pair.at[chain, step],
            send_sem=send_p.at[chain, step],
            recv_sem=recv_p.at[chain, step],
            device_id={"dp": other},
        )

    def ring_copy(chain, half, step):
        return pltpu.make_async_remote_copy(
            src_ref=held.at[chain, step, half],
            dst_ref=arrived.at[chain, step, half],
            send_sem=send_r.at[chain, step, half],
            recv_sem=recv_r.at[chain, step, half],
            device_id={"dp": up if chain < BLOCKS // 2 else down},
        )

    turn = [0, BLOCKS // 2, 1, BLOCKS // 2 + 1]
    for j in turn:
        for s in range(MOST):
            q = j * MOST + s
            pick = pick_ref[q]
            norm = jnp.sum(jnp.where(list_of == pick, norms, 0.0), axis=0, keepdims=True)
            prob = jnp.exp(scores[q] - norm)
            hot = (taxon == target_ref[q]).astype(jnp.float32)
            value = jnp.where(taxon + pick >= taxon, prob - hot, 0.0)
            probs[:, s * 128 : (s + 1) * 128] = value.astype(jnp.bfloat16)
        total = jnp.dot(
            probs[...],
            picked[j * MOST : (j + 1) * MOST].reshape(MOST * 128, picked.shape[2]),
            preferred_element_type=jnp.float32,
        )
        grad[j] = total.reshape(grad.shape[1:])
        for step in range(NZ):
            pair_copy(j, step).start()
    for step in range(NZ):
        for chain in turn:
            pair_copy(chain, step).wait_recv()
            for half in range(2):
                span = pl.ds(half * 8, 8)
                value = (
                    grad[chain, chunk_of(chain, step) * 2 + core, span, :]
                    + pair[chain, step, span, :]
                )
                if step > 0:
                    ring_copy(chain, half, step - 1).wait_recv()
                    value = value + arrived[chain, step - 1, half]
                if step < NZ - 1:
                    held[chain, step, half] = value
                    ring_copy(chain, half, step).start()
                else:
                    out_ref[chain, span, :] = value
    for step in range(NZ):
        for chain in turn:
            pair_copy(chain, step).wait_send()
            if step < NZ - 1:
                for half in range(2):
                    ring_copy(chain, half, step).wait_send()


def combine_and_scatter(stats, target, pick, scores, picked, shares):
    slots, taxa, _ = scores.shape
    width, share = picked.shape[2], taxa // shares
    vmem = pl.BlockSpec(memory_space=pltpu.VMEM)
    hbm = pl.BlockSpec(memory_space=pltpu.HBM)
    dma = pltpu.SemaphoreType.DMA
    return pl.pallas_call(
        grad_kernel,
        out_shape=[
            jax.ShapeDtypeStruct((N_CLS, 8, 128), jnp.float32),
            jax.ShapeDtypeStruct((BLOCKS, share, width), jnp.float32),
        ],
        in_specs=[vmem] * 3 + [hbm] * 2,
        out_specs=[vmem] * 2,
        scratch_shapes=[
            pltpu.VMEM((slots, taxa, 128), jnp.float32),
            pltpu.VMEM((slots, 128, width), jnp.bfloat16),
            pltpu.VMEM((N_CLS, 8, 128), jnp.float32),
            pltpu.VMEM((8, 128), jnp.float32),
            pltpu.VMEM((taxa, MOST * 128), jnp.bfloat16),
            pltpu.VMEM((BLOCKS, shares, share, width), jnp.float32),
            pltpu.VMEM((BLOCKS, NZ, share, width), jnp.float32),
            pltpu.VMEM((BLOCKS, NZ, 2, share // 2, width), jnp.float32),
            pltpu.VMEM((BLOCKS, NZ, 2, share // 2, width), jnp.float32),
            dma((N_CLS,)),
            dma((N_CLS,)),
            dma((N_CLS,)),
            dma((N_CLS,)),
            dma((BLOCKS, NZ)),
            dma((BLOCKS, NZ)),
            dma((BLOCKS, NZ, 2)),
            dma((BLOCKS, NZ, 2)),
            dma((2,)),
        ],
        compiler_params=pltpu.CompilerParams(
            collective_id=0, has_side_effects=True, vmem_limit_bytes=48 * 1024 * 1024
        ),
        name="combine_and_scatter",
    )(stats, target, pick, scores, picked)


def body(embeddings, class_rows, cand_blocks, label_pos):
    local_blocks, block_taxa, feature_width = class_rows.shape
    own_images, (own_lists, listed) = label_pos.shape[0], cand_blocks.shape
    small = jnp.concatenate([label_pos, cand_blocks.reshape(-1)])
    small = jnp.pad(small, (0, 8 * 128 - small.shape[0])).reshape(8, 128)
    gathered, small_all = gather_images(embeddings, small)
    gathered = gathered.reshape(N_CLS * own_images, feature_width)
    small_all = small_all.reshape(N_CLS, 8 * 128)
    labels_all = small_all[:, :own_images].reshape(-1)
    cand_all = small_all[:, own_images : own_images + own_lists * listed].reshape(-1, listed)
    group_lists = cand_all.shape[0]
    dp_images = gathered.shape[0]
    group_rows = dp_images // group_lists
    my_shard = lax.axis_index("cls")
    owned_ids = my_shard * local_blocks + jnp.arange(local_blocks, dtype=jnp.int32)
    matches = (cand_all[:, :, None] == owned_ids[None, None, :]).astype(jnp.int32)
    hit_count = jnp.sum(matches, axis=1)
    slot_of = jnp.sum(
        matches * jnp.arange(cand_all.shape[1], dtype=jnp.int32)[None, :, None], axis=1
    )
    hit_rank = jnp.cumsum(hit_count, axis=0) - 1
    slot_ids = jnp.arange(MOST, dtype=jnp.int32)
    chosen = (
        (hit_count[:, :, None] > 0) & (hit_rank[:, :, None] == slot_ids[None, None, :])
    ).astype(jnp.int32)
    block_index = jnp.arange(group_lists, dtype=jnp.int32)[:, None, None]
    src_block = jnp.sum(chosen * block_index, axis=0)
    valid_slot = jnp.sum(chosen, axis=0)
    src_slot = jnp.sum(chosen * slot_of[:, :, None], axis=0)
    valid = valid_slot.reshape(-1, 1) > 0
    label_tiles = labels_all.reshape(group_lists, group_rows)[src_block.reshape(-1)]
    target = jnp.where(valid, label_tiles - src_slot.reshape(-1, 1) * block_taxa, -1)
    pick = jnp.broadcast_to(jnp.where(valid, src_block.reshape(-1, 1), -1), target.shape)
    target, pick = target[:, None, :], pick[:, None, :]
    scores, picked, stats = score_slots(
        src_block.reshape(-1), gathered.reshape(group_lists, group_rows, feature_width), class_rows, target, pick
    )
    combined, grad = combine_and_scatter(stats, target, pick, scores, picked, lax.axis_size("dp"))
    per = group_lists // N_CLS
    image_loss = combined[:, per : 2 * per].reshape(dp_images)
    class_grad = grad.transpose(1, 0, 2)
    return (image_loss, class_grad)


def solution(mesh):
    in_specs = (
        P(("dp", "cls"), None),
        P("cls", None, None),
        P(("dp", "cls"), None),
        P(("dp", "cls")),
    )
    out_specs = (P("dp"), P("dp", "cls", None))
    return jax.shard_map(body, mesh=mesh, in_specs=in_specs, out_specs=out_specs, check_vma=False)
```

time: 183 us -> 170 us (0.929)
  Pallas kernels: 144 us -> 158 us
  matrix products: 13.6 us -> 0 us
  local copies, waits for them, and re-layouts: 16.5 us -> 8.74 us
  other arithmetic: 7.45 us -> 1.97 us
    pallas_call x2, Pallas kernels: 58.7 us -> 73 us  [the longest x1 56.2 us: combine_and_scatter(): pl.pallas_call(grad_kernel, out_shape=[jax.ShapeDtypeStruct((N_CLS, 8, 12...]
    dot_general x3 -> x0, matrix products: 13.6 us -> none  [the longest x1 6.74 us: body(): jnp.einsum('jsit,jsid->jtd', logit_grad, image_tiles, preferred_element_t...]
    gather x4 -> x1, local copies, waits for them, and re-layouts: 9.85 us -> 0.57 us  [body(): labels_all.reshape(group_lists, group_rows)[src_block.reshape(-1)]]
    reduce_sum x2 -> x1, other arithmetic: 5.17 us -> 0.3 us  [body(): src_slot = jnp.sum(chosen * slot_of[:, :, None], axis=0)]
    unnamed x4 -> x12, local copies, waits for them, and re-layouts: 2.67 us -> 4.83 us
where the time goes in v3:
time: 170 us; the launch traced here: 169 us
  Pallas kernels  158 us (93%)
  local copies, waits for them, and re-layouts  8.74 us (5%)
  other arithmetic  1.97 us (1%)
    pallas_call x1, Pallas kernels, gather_images(): pl.pallas_call(gather_kernel, out_shape=[jax.ShapeDtypeStruct((N_CLS, row...  85 us
    pallas_call x1, Pallas kernels, combine_and_scatter(): pl.pallas_call(grad_kernel, out_shape=[jax.ShapeDtypeStruct((N_CLS, 8, 12...  56.2 us
    pallas_call x1, Pallas kernels, score_slots(): pl.pallas_call(score_kernel, grid_spec=pltpu.PrefetchScalarGridSpec(num_s...  16.7 us
    unnamed x12, local copies, waits for them, and re-layouts  4.83 us

profile of v3, /device:TPU:8, one launch (start us, length us, event | category | flops | bytes accessed | tf_op | source)
XLA Modules:
  0.0 169.5 jit_solution(18074061423181231057)
XLA Ops:
  0.6 0.8 reshape.147
  1.4 0.7 pad_add_fusion
  2.1 0.6 pad_bitcast_fusion.small_ref
  2.7 85.0 %gather_images.1 = (bf16[32,256,768]{2,1,0:T(8,128)(2,1)}, s32[32,8,128]{2,1,0:T(8,128)}) custom-call(bf16[256,768]{1,0:T(8,128)(2,1)} %own_ref.1, s32[8,128]{1,0:T(8,128)} %pad_bitcast_fusion.small_ref), custom_call_target="tpu_custom_call" | custom-call | tf_op jit(solution)/shard_map/gather_images/pallas_call | solution.py:160
  87.7 0.9 copy.14
  88.7 0.1 eq.28
  88.8 0.1 copy.8
  88.8 0.1 fusion.1
  89.0 0.1 copy.9
  89.0 0.1 reduce_window_sum.11
  89.2 0.1 copy.10
  89.2 0.3 select_reduce_fusion
  89.5 0.1 mul.50
  89.6 0.1 reshape.150.src_ref
  89.7 0.0 copy-start.4
  89.7 0.1 reshape.151
  89.8 0.1 gt.34
  89.9 0.6 gather_fusion
  90.5 0.7 broadcast_select_fusion.target_ref
  91.2 0.7 broadcast_in_dim_broadcast_in_dim.2.pick_ref
  91.9 0.0 copy-done.4
  91.9 0.0 copy-start.1
  91.9 0.0 copy-start.2
  91.9 16.7 %score_slots.1 = (f32[32,256,128]{2,1,0:T(8,128)}, bf16[32,128,768]{2,1,0:T(8,128)(2,1)}, f32[32,8,128]{2,1,0:T(8,128)}) custom-call(s32[32]{0:T(128)} %copy-done.4, bf16[64,128,768]{2,1,0:T(8,128)(2,1)} %bitcast.13, bf16[64,128,768]{2,1,0:T(8,128)(2,1)} %bitcast.14, bf16[4,256,768]{2,1,0:T(8,128)(2,1)} %rows_ref.1, ...), custom_call_target="tpu_custom_call" | custom-call | tf_op jit(solution)/shard_map/score_slots/pallas_call | solution.py:232
  108.7 0.0 copy-done.1
  108.7 0.0 copy-done.2
  108.7 0.0 copy-start
  108.7 2.2 %copy-done = f32[32,256,128]{2,1,0:T(8,128)S(1)} copy-done((f32[32,256,128]{2,1,0:T(8,128)S(1)}, f32[32,256,128]{2,1,0:T(8,128)}, u32[]{:S(2)}) %copy-start) | copy-done | bytes 4194328
  110.9 0.9 copy-done.3
  111.8 56.2 %combine_and_scatter.1 = (f32[32,8,128]{2,1,0:T(8,128)S(1)}, f32[4,16,768]{2,1,0:T(8,128)S(1)}) custom-call(f32[32,8,128]{2,1,0:T(8,128)S(1)} %copy-done.3, s32[32,1,128]{2,1,0:T(1,128)S(1)} %copy-done.1, s32[32,1,128]{2,1,0:T(1,128)S(1)} %copy-done.2, f32[32,256,128]{2,1,0:T(8,128)S(1)} %copy-done, bf16[32,128,768]{2,1,0:T(8,128)(2,1)} %get-tuple-element.13.picked_in), custom_call_target="tpu_custom_call" | custom-call | tf_op jit(solution)/shard_map/combine_and_scatter/pallas_call | solution.py:416
  168.0 0.6 slice.11
  168.7 0.8 copy.11
  (12 shorter events, 0.1 us)
Async XLA Ops:
  89.7 2.2 %copy-start.4 = (s32[32]{0:T(128)}, s32[32]{0:T(128)S(1)}, u32[]{:S(2)}) copy-start(s32[32]{0:T(128)S(1)} %reshape.150.src_ref) | copy-start | bytes 388
  91.9 16.7 %copy-start.1 = (s32[32,1,128]{2,1,0:T(1,128)S(1)}, s32[32,1,128]{2,1,0:T(1,128)}, u32[]{:S(2)}) copy-start(s32[32,1,128]{2,1,0:T(1,128)} %broadcast_select_fusion.target_ref) | copy-start | bytes 49156
  91.9 16.8 %copy-start.2 = (s32[32,1,128]{2,1,0:T(1,128)S(1)}, s32[32,1,128]{2,1,0:T(1,128)}, u32[]{:S(2)}) copy-start(s32[32,1,128]{2,1,0:T(1,128)} %broadcast_in_dim_broadcast_in_dim.2.pick_ref) | copy-start | bytes 49156
  108.7 2.2 %copy-start = (f32[32,256,128]{2,1,0:T(8,128)S(1)}, f32[32,256,128]{2,1,0:T(8,128)}, u32[]{:S(2)}) copy-start(f32[32,256,128]{2,1,0:T(8,128)} %get-tuple-element.12.scores_in) | copy-start | bytes 12582916
  110.9 0.9 copy-start.3

commit v4 on v3

--- a/solution.py
+++ b/solution.py
@@ -11,7 +11,7 @@
 
 
 NX, NY, NZ = 4, 8, 8
-A_ROWS = 96
+A_ROWS = 104
 BLOCKS = 4
 
 
@@ -26,10 +26,10 @@
         size, start = (a_rows, 0) if kind == "A" else (b_rows, a_rows)
         first, second = (u, v) if kind == "A" else (v, u)
         far1, far2 = (NX // 2, NY // 2) if kind == "A" else (NY // 2, NX // 2)
-        if abs(first) == far1:
-            return (start, size // 2) if first < 0 else (start + size // 2, size // 2)
-        if abs(second) == far2:
-            return (start, size // 2) if second < 0 else (start + size // 2, size // 2)
+        if abs(first) == far1 or abs(second) == far2:
+            before = first if abs(first) == far1 else second
+            lower = -(-size // 16) * 8
+            return (start, lower) if before < 0 else (start + lower, size - lower)
         return start, size
 
     def sends(kind, u, v, came):
@@ -177,28 +177,34 @@
     )(embeddings, small)
 
 
-def score_kernel(src_ref, one_ref, two_ref, rows_ref, target_ref, pick_ref, scores_ref, picked_ref, stats_ref, slot_stats):
+def score_kernel(src_ref, *refs):
     del src_ref
+    image_refs = refs[:MOST]
+    rows_ref, target_ref, pick_ref, scores_ref, picked_ref, stats_ref, slot_stats = refs[MOST:]
     p = pl.program_id(0)
-    picked_ref[0] = one_ref[0]
-    picked_ref[1] = two_ref[0]
-    both = jnp.concatenate([one_ref[0], two_ref[0]], axis=0)
-    score = lax.dot_general(
-        rows_ref[0], both, (((1,), (1,)), ((), ())), preferred_element_type=jnp.float32
-    )
     taxon = lax.broadcasted_iota(jnp.int32, (256, 128), 0)
-    for i in range(2):
-        part = score[:, i * 128 : (i + 1) * 128]
-        scores_ref[i] = part
-        top = jnp.max(part, axis=0, keepdims=True)
-        q = 2 * p + i
-        slot_stats[q, 0:1, :] = top
-        slot_stats[q, 1:2, :] = jnp.sum(jnp.exp(part - top), axis=0, keepdims=True)
-        slot_stats[q, 2:3, :] = jnp.sum(
-            jnp.where(taxon == target_ref[i], part, 0.0), axis=0, keepdims=True
-        )
-
-    @pl.when(p == BLOCKS * MOST // 2 - 1)
+    for first in range(0, MOST, 2):
+        pair = [image_refs[first][0], image_refs[first + 1][0]]
+        picked_ref[first] = pair[0]
+        picked_ref[first + 1] = pair[1]
+        score = lax.dot_general(
+            rows_ref[0],
+            jnp.concatenate(pair, axis=0),
+            (((1,), (1,)), ((), ())),
+            preferred_element_type=jnp.float32,
+        )
+        for i in range(2):
+            part = score[:, i * 128 : (i + 1) * 128]
+            scores_ref[first + i] = part
+            top = jnp.max(part, axis=0, keepdims=True)
+            q = MOST * p + first + i
+            slot_stats[q, 0:1, :] = top
+            slot_stats[q, 1:2, :] = jnp.sum(jnp.exp(part - top), axis=0, keepdims=True)
+            slot_stats[q, 2:3, :] = jnp.sum(
+                jnp.where(taxon == target_ref[first + i], part, 0.0), axis=0, keepdims=True
+            )
+
+    @pl.when(p == BLOCKS - 1)
     def merge():
         list_of = lax.broadcasted_iota(jnp.int32, (2 * N_CLS, 128), 0)
 
@@ -233,17 +239,19 @@
         score_kernel,
         grid_spec=pltpu.PrefetchScalarGridSpec(
             num_scalar_prefetch=1,
-            grid=(slots // 2,),
+            grid=(BLOCKS,),
             in_specs=[
-                pl.BlockSpec((1, 128, width), lambda p, src: (src[2 * p], 0, 0)),
-                pl.BlockSpec((1, 128, width), lambda p, src: (src[2 * p + 1], 0, 0)),
-                pl.BlockSpec((1, taxa, width), lambda p, src: (p // (MOST // 2), 0, 0)),
-                pl.BlockSpec((2, 1, 128), lambda p, src: (p, 0, 0)),
+                *[
+                    pl.BlockSpec((1, 128, width), lambda p, src, i=i: (src[MOST * p + i], 0, 0))
+                    for i in range(MOST)
+                ],
+                pl.BlockSpec((1, taxa, width), lambda p, src: (p, 0, 0)),
+                pl.BlockSpec((MOST, 1, 128), lambda p, src: (p, 0, 0)),
                 pl.BlockSpec((slots, 1, 128), lambda p, src: (0, 0, 0)),
             ],
             out_specs=[
-                pl.BlockSpec((2, taxa, 128), lambda p, src: (p, 0, 0)),
-                pl.BlockSpec((2, 128, width), lambda p, src: (p, 0, 0)),
+                pl.BlockSpec((MOST, taxa, 128), lambda p, src: (p, 0, 0)),
+                pl.BlockSpec((MOST, 128, width), lambda p, src: (p, 0, 0)),
                 pl.BlockSpec((N_CLS, 8, 128), lambda p, src: (0, 0, 0)),
             ],
             scratch_shapes=[pltpu.VMEM((slots, 8, 128), jnp.float32)],
@@ -254,7 +262,7 @@
             jax.ShapeDtypeStruct((N_CLS, 8, 128), jnp.float32),
         ],
         name="score_slots",
-    )(src, images, images, class_rows, target, pick)
+    )(src, *([images] * MOST), class_rows, target, pick)
 
 
 def grad_kernel(
@@ -442,7 +450,7 @@
             dma((2,)),
         ],
         compiler_params=pltpu.CompilerParams(
-            collective_id=0, has_side_effects=True, vmem_limit_bytes=48 * 1024 * 1024
+            collective_id=0, has_side_effects=True, vmem_limit_bytes=62 * 1024 * 1024
         ),
         name="combine_and_scatter",
     )(stats, target, pick, scores, picked)

time: 170 us -> 166 us (0.976)
  Pallas kernels: 158 us -> 155 us
    pallas_call x1, Pallas kernels: 16.7 us -> 9.85 us  [score_slots(): pl.pallas_call(score_kernel, grid_spec=pltpu.PrefetchScalarGridSpec(num_s...]
    pallas_call x1, Pallas kernels: 56.2 us -> 58.8 us  [combine_and_scatter(): pl.pallas_call(grad_kernel, out_shape=[jax.ShapeDtypeStruct((N_CLS, 8, 12...]
    unnamed x12 -> x4, local copies, waits for them, and re-layouts: 4.83 us -> 2.66 us
    pallas_call x1, Pallas kernels: 85 us -> 86.8 us  [gather_images(): pl.pallas_call(gather_kernel, out_shape=[jax.ShapeDtypeStruct((N_CLS, row...]
where the time goes in v4:
time: 166 us
  Pallas kernels  155 us (93%)
  local copies, waits for them, and re-layouts  7.48 us (5%)
  other arithmetic  1.97 us (1%)
    pallas_call x1, Pallas kernels, gather_images(): pl.pallas_call(gather_kernel, out_shape=[jax.ShapeDtypeStruct((N_CLS, row...  86.8 us
    pallas_call x1, Pallas kernels, combine_and_scatter(): pl.pallas_call(grad_kernel, out_shape=[jax.ShapeDtypeStruct((N_CLS, 8, 12...  58.8 us
    pallas_call x1, Pallas kernels, score_slots(): pl.pallas_call(score_kernel, grid_spec=pltpu.PrefetchScalarGridSpec(num_s...  9.85 us

profile of v4, /device:TPU:8, one launch (start us, length us, event | category | flops | bytes accessed | tf_op | source)
XLA Modules:
  0.0 165.6 jit_solution(8236480267972328864)
XLA Ops:
  0.6 0.8 reshape.147
  1.4 0.7 pad_add_fusion
  2.1 0.6 pad_bitcast_fusion.small_ref
  2.7 86.8 %gather_images.1 = (bf16[32,256,768]{2,1,0:T(8,128)(2,1)}, s32[32,8,128]{2,1,0:T(8,128)}) custom-call(bf16[256,768]{1,0:T(8,128)(2,1)} %own_ref.1, s32[8,128]{1,0:T(8,128)} %pad_bitcast_fusion.small_ref), custom_call_target="tpu_custom_call" | custom-call | tf_op jit(solution)/shard_map/gather_images/pallas_call | solution.py:160
  89.5 0.9 copy.14
  90.4 0.1 eq.28
  90.5 0.1 copy.8
  90.6 0.1 fusion.1
  90.7 0.1 copy.9
  90.8 0.1 reduce_window_sum.11
  90.9 0.1 copy.10
  91.0 0.3 select_reduce_fusion
  91.3 0.1 mul.50
  91.4 0.1 reshape.150.src_ref
  91.4 0.0 copy-start
  91.4 0.1 reshape.151
  91.5 0.1 gt.34
  91.6 0.6 gather_fusion
  92.2 0.7 broadcast_select_fusion.refs_9_.target_ref
  93.0 0.7 broadcast_in_dim_broadcast_in_dim.2.refs_10_.pick_ref
  93.7 0.0 copy-done
  93.7 9.8 %score_slots.1 = (f32[32,256,128]{2,1,0:T(8,128)}, bf16[32,128,768]{2,1,0:T(8,128)(2,1)}, f32[32,8,128]{2,1,0:T(8,128)}) custom-call(s32[32]{0:T(128)} %copy-done, bf16[64,128,768]{2,1,0:T(8,128)(2,1)} %bitcast.12, bf16[64,128,768]{2,1,0:T(8,128)(2,1)} %bitcast.13, bf16[64,128,768]{2,1,0:T(8,128)(2,1)} %bitcast.14, bf16[64,128,768]{2,1,0:T(8,128)(2,1)} %bitcast.15, ...), custom_call_target="tpu_custom_call" | custom-call | tf_op jit(solution)/shard_map/score_slots/pallas_call | solution.py:238
  103.5 58.8 %combine_and_scatter.1 = (f32[32,8,128]{2,1,0:T(8,128)}, f32[4,16,768]{2,1,0:T(8,128)}) custom-call(f32[32,8,128]{2,1,0:T(8,128)} %get-tuple-element.11.stats, s32[32,1,128]{2,1,0:T(1,128)} %broadcast_select_fusion.refs_9_.target_ref, s32[32,1,128]{2,1,0:T(1,128)} %broadcast_in_dim_broadcast_in_dim.2.refs_10_.pick_ref, ...), custom_call_target="tpu_custom_call" | custom-call | tf_op jit(solution)/shard_map/combine_and_scatter/pallas_call | solution.py:424
  162.3 1.5 slice.11
  163.8 1.7 %copy.11 = f32[16,4,768]{2,1,0:T(4,128)} copy(f32[16,4,768]{2,0,1:T(8,128)} %bitcast.22) | data formatting | bytes 393216
  (11 shorter events, 0.1 us)
Async XLA Ops:
  91.4 2.2 %copy-start = (s32[32]{0:T(128)}, s32[32]{0:T(128)S(1)}, u32[]{:S(2)}) copy-start(s32[32]{0:T(128)S(1)} %reshape.150.src_ref) | copy-start | bytes 388

commit v5 on v4

--- a/solution.py
+++ b/solution.py
@@ -11,7 +11,7 @@
 
 
 NX, NY, NZ = 4, 8, 8
-A_ROWS = 104
+A_ROWS = 96
 BLOCKS = 4
 
 

time: 166 us -> 163 us (0.982)
  Pallas kernels: 155 us -> 152 us
    pallas_call x1, Pallas kernels: 86.8 us -> 85 us  [gather_images(): pl.pallas_call(gather_kernel, out_shape=[jax.ShapeDtypeStruct((N_CLS, row...]
where the time goes in v5:
time: 163 us
  Pallas kernels  152 us (93%)
  local copies, waits for them, and re-layouts  7.48 us (5%)
  other arithmetic  1.97 us (1%)
    pallas_call x1, Pallas kernels, gather_images(): pl.pallas_call(gather_kernel, out_shape=[jax.ShapeDtypeStruct((N_CLS, row...  85 us
    pallas_call x1, Pallas kernels, combine_and_scatter(): pl.pallas_call(grad_kernel, out_shape=[jax.ShapeDtypeStruct((N_CLS, 8, 12...  57.3 us
    pallas_call x1, Pallas kernels, score_slots(): pl.pallas_call(score_kernel, grid_spec=pltpu.PrefetchScalarGridSpec(num_s...  10 us

profile of v5, /device:TPU:8, one launch (start us, length us, event | category | flops | bytes accessed | tf_op | source)
XLA Modules:
  0.0 162.5 jit_solution(9998978698923119959)
XLA Ops:
  0.6 0.8 reshape.147
  1.4 0.7 pad_add_fusion
  2.1 0.6 pad_bitcast_fusion.small_ref
  2.7 85.0 %gather_images.1 = (bf16[32,256,768]{2,1,0:T(8,128)(2,1)}, s32[32,8,128]{2,1,0:T(8,128)}) custom-call(bf16[256,768]{1,0:T(8,128)(2,1)} %own_ref.1, s32[8,128]{1,0:T(8,128)} %pad_bitcast_fusion.small_ref), custom_call_target="tpu_custom_call" | custom-call | tf_op jit(solution)/shard_map/gather_images/pallas_call | solution.py:160
  87.7 0.9 copy.14
  88.7 0.1 eq.28
  88.8 0.1 copy.8
  88.8 0.1 fusion.1
  89.0 0.1 copy.9
  89.0 0.1 reduce_window_sum.11
  89.2 0.1 copy.10
  89.2 0.3 select_reduce_fusion
  89.5 0.1 mul.50
  89.6 0.1 reshape.150.src_ref
  89.7 0.0 copy-start
  89.7 0.1 reshape.151
  89.8 0.1 gt.34
  89.9 0.6 gather_fusion
  90.5 0.7 broadcast_select_fusion.refs_9_.target_ref
  91.2 0.7 broadcast_in_dim_broadcast_in_dim.2.refs_10_.pick_ref
  91.9 0.0 copy-done
  91.9 10.0 %score_slots.1 = (f32[32,256,128]{2,1,0:T(8,128)}, bf16[32,128,768]{2,1,0:T(8,128)(2,1)}, f32[32,8,128]{2,1,0:T(8,128)}) custom-call(s32[32]{0:T(128)} %copy-done, bf16[64,128,768]{2,1,0:T(8,128)(2,1)} %bitcast.12, bf16[64,128,768]{2,1,0:T(8,128)(2,1)} %bitcast.13, bf16[64,128,768]{2,1,0:T(8,128)(2,1)} %bitcast.14, bf16[64,128,768]{2,1,0:T(8,128)(2,1)} %bitcast.15, ...), custom_call_target="tpu_custom_call" | custom-call | tf_op jit(solution)/shard_map/score_slots/pallas_call | solution.py:238
  101.9 57.3 %combine_and_scatter.1 = (f32[32,8,128]{2,1,0:T(8,128)}, f32[4,16,768]{2,1,0:T(8,128)}) custom-call(f32[32,8,128]{2,1,0:T(8,128)} %get-tuple-element.11.stats, s32[32,1,128]{2,1,0:T(1,128)} %broadcast_select_fusion.refs_9_.target_ref, s32[32,1,128]{2,1,0:T(1,128)} %broadcast_in_dim_broadcast_in_dim.2.refs_10_.pick_ref, ...), custom_call_target="tpu_custom_call" | custom-call | tf_op jit(solution)/shard_map/combine_and_scatter/pallas_call | solution.py:424
  159.3 1.5 slice.11
  160.8 1.7 %copy.11 = f32[16,4,768]{2,1,0:T(4,128)} copy(f32[16,4,768]{2,0,1:T(8,128)} %bitcast.22) | data formatting | bytes 393216
  (11 shorter events, 0.1 us)
Async XLA Ops:
  89.7 2.2 %copy-start = (s32[32]{0:T(128)}, s32[32]{0:T(128)S(1)}, u32[]{:S(2)}) copy-start(s32[32]{0:T(128)S(1)} %reshape.150.src_ref) | copy-start | bytes 388
